TPU v7x, 512 devices: a whole 4x8x8 slice. The times are simulated.
512 devices in a mesh: rep: 4 (over y_hi, core), sp: 128 (over y_lo, z, x).
Axes of the slice: x: 4, y: 8 (y_hi: 2, y_lo: 4; y = y_hi * 4 + y_lo), z: 8, core: 2. Of those that a mesh axis runs over, the one named last changes fastest.
Arguments:
- film_start: float32 [4, 2048, 2048], P('rep', 'sp'), may hold values from 0.2 to 2
- evaporation: float32 [4, 2048, 2048], P('rep', 'sp'), may hold values from 0.05 to 0.5
- contact_mask: int32 [4, 2048, 2048], P('rep', 'sp'), may hold values 0 or 1
- first_classes: int32 [4, 2048, 16], P('rep'), may hold values from 0 to 3
- second_classes: int32 [4, 2048, 16], P('rep', 'sp'), may hold values from 0 to 3
- span_inverses: float32 [4, 128, 128], replicated, may hold values from -0.4 to 1
- conv_weight: bfloat16 [3, 3, 4, 64], replicated, may hold values from -0.5 to 0.5
- mixing_weight: bfloat16 [64, 64], replicated, may hold values from -0.75 to 0.75
- flux_weight: bfloat16 [64], replicated, may hold values from -0.75 to 0.75
- film_cotangent: float32 [4, 2048, 2048], P('rep', 'sp'), may hold values from -6 to 6
Outputs:
- final_film: float32 [4, 2048, 2048], P('rep', 'sp')
- film_grad: float32 [4, 2048, 2048], P('rep', 'sp')
- conv_grad: float32 [3, 3, 4, 64], replicated
- mixing_grad: float32 [64, 64], replicated
- flux_grad: float32 [64], replicated
All inputs are finite; a program needn't handle non-finite values. No bound on the sum of `contact_mask` on one device may be relied on, other than what follows from the above.
Results may differ from a plain program's by a relative error of at most 0.019.
Values may be sent and summed in bfloat16 or wider, within the bound.
A program may use at most 128 MiB of HBM per device.

v0:
```python
from functools import partial
import math
import jax
import jax.numpy as jnp
from jax import lax
from jax.sharding import PartitionSpec as P

STEPS = 1
time_step = 0.5


def extended(array, sides, width):
    for axis, dim in sides:
        size, length = (lax.axis_size(axis), array.shape[dim])
        up = [(i, (i + 1) % size) for i in range(size - 1)]
        down = [(j, i) for i, j in up]
        last = lax.slice_in_dim(array, length - width, length, axis=dim)
        first = lax.slice_in_dim(array, 0, width, axis=dim)
        before = lax.ppermute(last, axis, up)
        after = lax.ppermute(first, axis, down)
        array = jnp.concatenate([before, array, after], axis=dim)
    return array


def select_product(tile_rows, matrix, hits, current):
    product = jnp.dot(tile_rows, matrix, precision=lax.Precision.HIGHEST)
    return jnp.where(hits[:, None], product, current)


def keep_same(current):
    return current


def apply_spans(vectors, classes, inverses, transpose):
    count = vectors.shape[0]
    tile_size = math.gcd(128, count)
    line_order = jnp.argsort(classes, stable=True)
    ordered = jnp.take(vectors, line_order, axis=0)
    ordered_cls = jnp.take(classes, line_order)
    results = []
    for start in range(0, count, tile_size):
        tile_rows = ordered[start : start + tile_size]
        tile_cls = ordered_cls[start : start + tile_size]
        result = jnp.zeros_like(tile_rows)
        for group in range(inverses.shape[0]):
            matrix = inverses[group] if transpose else inverses[group].T
            hits = tile_cls == group
            result = lax.cond(
                jnp.any(hits), partial(select_product, tile_rows, matrix, hits), keep_same, result
            )
        results.append(result)
    joined = jnp.concatenate(results, axis=0)
    return jnp.zeros_like(vectors).at[line_order].set(joined)


def solve_lines(lines, classes, inverses, transpose):
    span = inverses.shape[1]
    vectors = lines.reshape(-1, span)
    return apply_spans(vectors, classes.reshape(-1), inverses, transpose).reshape(lines.shape)


def relayout(field):
    moved = lax.all_to_all(field, "sp", split_axis=2, concat_axis=1, tiled=True)
    return jnp.swapaxes(moved, 1, 2)


def split_columns(padded, width):
    count = (padded.shape[-1] - 2) // width
    return jnp.stack(
        [padded[..., number * width : number * width + width + 2] for number in range(count)]
    )


def join_blocks(blocks):
    moved = jnp.moveaxis(blocks, 0, -2)
    return moved.reshape(moved.shape[:-2] + (moved.shape[-2] * moved.shape[-1],))


def cut_blocks(field, width):
    shape = field.shape
    reshaped = field.reshape(shape[:-1] + (shape[-1] // width, width))
    return jnp.moveaxis(reshaped, -2, 0)


def join_padded(blocks):
    middle = jnp.moveaxis(blocks[..., 1:-1], 0, -2)
    left = jnp.moveaxis(blocks[..., 0], 0, -1)
    right = jnp.moveaxis(blocks[..., -1], 0, -1)
    middle = middle.at[..., :-1, -1].add(left[..., 1:])
    middle = middle.at[..., 1:, 0].add(right[..., :-1])
    return middle.reshape(middle.shape[:-2] + (middle.shape[-2] * middle.shape[-1],))


def tap_stack(piece):
    rows = piece.shape[2] - 2
    cols = piece.shape[3] - 2
    return jnp.concatenate(
        [
            piece[:, :, row_tap : row_tap + rows, col_tap : col_tap + cols]
            for row_tap in range(3)
            for col_tap in range(3)
        ],
        axis=0,
    )


def closure_forward(piece, conv_w, mixing_w, flux_w):
    stacked = tap_stack(piece)
    conv_matrix = conv_w.reshape(-1, conv_w.shape[-1])
    first_tanh = jnp.tanh(
        jnp.einsum("ko,krxy->orxy", conv_matrix, stacked, preferred_element_type=jnp.float32)
    )
    first_act = first_tanh.astype(jnp.bfloat16)
    second_tanh = jnp.tanh(
        jnp.einsum("op,orxy->prxy", mixing_w, first_act, preferred_element_type=jnp.float32)
    )
    second_act = second_tanh.astype(jnp.bfloat16)
    flux = jnp.einsum("p,prxy->rxy", flux_w, second_act, preferred_element_type=jnp.float32)
    return (flux, first_tanh, first_act, second_tanh, second_act, stacked)


def closure_backward(piece, flux_cot, conv_w, mixing_w, flux_w):
    rows = piece.shape[2] - 2
    cols = piece.shape[3] - 2
    channels = piece.shape[0]
    flux, first_tanh, first_act, second_tanh, second_act, stacked = closure_forward(
        piece, conv_w, mixing_w, flux_w
    )
    flux_part = jnp.einsum("prxy,rxy->p", second_act, flux_cot, preferred_element_type=jnp.float32)
    second_cot = (flux_w.astype(jnp.float32)[:, None, None, None] * flux_cot[None]).astype(
        jnp.bfloat16
    )
    pre_second_cot = second_cot * (1.0 - second_tanh * second_tanh)
    mixing_part = jnp.einsum(
        "orxy,prxy->op", first_act, pre_second_cot, preferred_element_type=jnp.float32
    )
    first_cot = jnp.einsum(
        "op,prxy->orxy", mixing_w, pre_second_cot, preferred_element_type=jnp.float32
    ).astype(jnp.bfloat16)
    pre_first_cot = first_cot * (1.0 - first_tanh * first_tanh)
    conv_part = jnp.einsum(
        "orxy,krxy->ko", pre_first_cot, stacked, preferred_element_type=jnp.float32
    ).reshape(conv_w.shape)
    conv_matrix = conv_w.reshape(-1, conv_w.shape[-1])
    tap_cots = jnp.einsum(
        "ko,orxy->krxy", conv_matrix, pre_first_cot, preferred_element_type=jnp.float32
    )
    piece_cot = jnp.zeros(piece.shape, jnp.float32)
    for row_tap in range(3):
        for col_tap in range(3):
            number = row_tap * 3 + col_tap
            term = tap_cots[number * channels : (number + 1) * channels]
            piece_cot = piece_cot.at[:, :, row_tap : row_tap + rows, col_tap : col_tap + cols].add(
                term
            )
    edges = jnp.stack([pre_first_cot[:, :, 0], pre_first_cot[:, :, -1]], axis=2)
    return (piece_cot, conv_part, mixing_part, flux_part, edges)


def rim_terms(neighbour, conv_w, row_tap, cols):
    padded = jnp.pad(neighbour, ((0, 0), (0, 0), (1, 1)))
    total = None
    for col_tap in range(3):
        term = jnp.einsum(
            "co,ory->cry",
            conv_w[row_tap, col_tap],
            padded[:, :, 2 - col_tap : 2 - col_tap + cols],
            preferred_element_type=jnp.float32,
        )
        total = term if total is None else total + term
    return total


def on_device(
    film_start,
    evaporation,
    contact_mask,
    first_classes,
    second_classes,
    span_inverses,
    conv_weight,
    mixing_weight,
    flux_weight,
    film_cotangent,
):
    maskf = contact_mask.astype(jnp.float32)
    side = film_start.shape[2]
    side_dev = film_start.shape[1]
    nspan = first_classes.shape[2]
    sp_index = lax.axis_index("sp")
    block_width = min(512, side)

    def first_solve(field, transpose):
        own_first = lax.dynamic_slice(
            first_classes, (0, sp_index * side_dev, 0), (1, side_dev, nspan)
        )
        solved = solve_lines(relayout(field), own_first, span_inverses, transpose)
        return relayout(solved)

    def forward_block(piece):
        return closure_forward(piece, conv_weight, mixing_weight, flux_weight)[0]

    def backward_block(items):
        return closure_backward(items[0], items[1], conv_weight, mixing_weight, flux_weight)

    height = film_start
    step = 0
    features = jnp.stack([height, height * height, maskf, evaporation]).astype(jnp.bfloat16)
    rimmed = extended(features, (("sp", 2),), 1)
    padded = jnp.pad(rimmed, ((0, 0), (0, 0), (0, 0), (1, 1)))
    pieces = split_columns(padded, block_width)
    flux = join_blocks(lax.map(forward_block, pieces))
    source_side = height + time_step * (flux - maskf * evaporation)
    across = first_solve(source_side, False)
    saved = [(height, pieces)]
    height = solve_lines(across, second_classes, span_inverses, False)
    final_film = height
    grad = film_cotangent
    conv_total = jnp.zeros(conv_weight.shape, jnp.float32)
    mixing_total = jnp.zeros(mixing_weight.shape, jnp.float32)
    flux_total = jnp.zeros(flux_weight.shape, jnp.float32)
    for step in reversed(range(STEPS)):
        height, pieces = saved[step]
        back = solve_lines(grad, second_classes, span_inverses, True)
        source_grad = first_solve(back, True)
        flux_cot = cut_blocks(time_step * source_grad, block_width)
        piece_cots, conv_parts, mixing_parts, flux_parts, edges = lax.map(
            backward_block, (pieces, flux_cot)
        )
        conv_total = jnp.sum(conv_parts, axis=0)
        mixing_total = jnp.sum(mixing_parts, axis=0)
        flux_total = jnp.sum(flux_parts, axis=0)
        whole = join_padded(piece_cots)
        inner = whole[:, :, 1:-1]
        rims = extended(join_blocks(edges).astype(jnp.bfloat16), (("sp", 2),), 1).astype(
            jnp.float32
        )
        inner = inner.at[:, :, 0].add(rim_terms(rims[:, :, 0], conv_weight, 2, side))
        inner = inner.at[:, :, -1].add(rim_terms(rims[:, :, 3], conv_weight, 0, side))
        feature_cot = inner.astype(jnp.bfloat16)
        grad = source_grad + feature_cot[0] + 2.0 * height * feature_cot[1]
    conv_sum, mixing_sum, flux_sum = lax.psum((conv_total, mixing_total, flux_total), ("rep", "sp"))
    scale = 1.0 / math.sqrt(lax.axis_size("rep") * film_start.shape[0] * side * side)
    return (final_film, grad, conv_sum * scale, mixing_sum * scale, flux_sum * scale)


def solution(mesh):
    return jax.shard_map(
        on_device,
        mesh=mesh,
        in_specs=(
            P("rep", "sp", None),
            P("rep", "sp", None),
            P("rep", "sp", None),
            P("rep", None, None),
            P("rep", "sp", None),
            P(),
            P(),
            P(),
            P(),
            P("rep", "sp", None),
        ),
        out_specs=(P("rep", "sp", None), P("rep", "sp", None), P(), P(), P()),
        check_vma=False,
    )
```

profile of v0, /device:TPU:2, one launch (start us, length us, event | category | flops | bytes accessed | tf_op | source)
XLA Modules:
  0.0 486.8 jit_solution(13716353377885899539)
XLA Ops:
  3.0 3.4 collective-permute-start
  6.4 5.7 %collective-permute-start.1 = (bf16[4,1,1,2048]{3,2,1,0:T(2,128)(2,1)S(1)}, bf16[4,1,1,2048]{3,2,1,0:T(2,128)(2,1)S(1)}, u32[]{:S(2)}, u32[]{:S(2)}) collective-permute-start(bf16[4,1,1,2048]{3,2,1,0:T(2,128)(2,1)S(1)} %get-tuple-element.1389), channel_id=1, source_target_pairs={{1,0},{2,1},{3,2},{4,3},{5,4},{6,5},{7,6},{8,7},{9,8},{10,9},{11,1... | collective-permute-start | bytes 49160 | tf_op jit(solution)/shard_map/ppermute | solution.py:20
  13.1 3.2 sort.35
  16.3 3.2 sort.36
  35.1 9.3 %reduce.65 = f32[2048,16]{1,0:T(8,128)S(1)} reduce(f32[2048,1,16]{2,1,0:T(1,128)S(1)} %bitcast.494, f32[]{:T(128)} %broadcast.556), dimensions={1}, to_apply=%bitcast.318.reduce_sub_computation | reduce | bytes 262148
  45.5 15.7 %all-to-all-start.2 = ((f32[128,1,256]{2,1,0:T(1,128)}), f32[128,1,256]{2,1,0:T(1,128)S(1)}, u32[]{:S(2)}, u32[]{:S(2)}) async-start(f32[128,1,256]{2,1,0:T(1,128)} %reshape.1187), calls=%async_computation.2 | async-start | bytes 262144 | tf_op jit(solution)/shard_map/all_to_all | solution.py:63
  83.1 9.3 %reduce.67 = f32[2048,16]{1,0:T(8,128)S(1)} reduce(f32[2048,1,16]{2,1,0:T(1,128)S(1)} %bitcast.495, f32[]{:T(128)} %broadcast.556), dimensions={1}, to_apply=%bitcast.320.reduce_sub_computation | reduce | bytes 262148
  93.5 13.1 %all-to-all-start.3 = ((f32[128,1,256]{2,1,0:T(1,128)}), f32[128,1,256]{2,1,0:T(1,128)S(1)}, u32[]{:S(2)}, u32[]{:S(2)}) async-start(f32[128,1,256]{2,1,0:T(1,128)} %reshape.1189), calls=%async_computation.3 | async-start | bytes 262144 | tf_op jit(solution)/shard_map/all_to_all | solution.py:63
  106.6 7.4 %while.44 = (s32[]{:T(128)}, f32[4,1,16,512]{3,2,1,0:T(8,128)S(1)}, bf16[4,4,1,18,514]{4,1,3,2,0:T(4,128)(2,1)S(1)}, bf16[3,3,4,64]{3,2,1,0:T(4,128)(2,1)S(1)}, ...) while((s32[]{:T(128)}, f32[4,1,16,512]{3,2,1,0:T(8,128)S(1)}, ...), condition=%wide.region_11.13_spmd, body=%wide.region_10.12_spmd.sunk | while | flops 106954752 | bytes 5314845 | solution.py:212
  124.8 156.3 %while.45 = (s32[]{:T(128)}, f32[4,4,1,18,514]{4,1,3,2,0:T(4,128)}, f32[4,3,3,4,64]{4,3,2,1,0:T(4,128)}, f32[4,64,64]{2,1,0:T(8,128)}, f32[4,64]{1,0:T(4,128)}, ...) while((s32[]{:T(128)}, f32[4,4,1,18,514]{4,1,3,2,0:T(4,128)}, ...), condition=%wide.region_90.93_spmd, body=%wide.region_88.92_spmd.sunk | while | flops 327188544 | bytes 51537856 | solution.py:227
  133.3 3.1 fusion.288
  141.4 4.0 scatter-add.90
  147.5 4.0 scatter-add.91
  172.4 3.1 fusion.288
  180.5 4.0 scatter-add.90
  186.5 4.0 scatter-add.91
  211.4 3.1 fusion.288
  219.5 4.0 scatter-add.90
  225.5 4.0 scatter-add.91
  250.4 3.1 fusion.288
  258.5 4.0 scatter-add.90
  264.5 4.0 scatter-add.91
  281.1 4.8 copy.228
  286.5 5.3 %fusion.141 = (f32[4,4,1,18,512]{3,1,0,4,2:T(4,128)S(1)}, f32[4,1,18,4,512]{2,0,3,4,1:T(4,128)}) fusion(f32[4,4,1,18,514]{3,1,0,4,2:T(4,128)} %copy.228), kind=kLoop, calls=%fused_computation.279 | loop fusion | bytes 1769472 | tf_op jit(solution)/shard_map/slice | solution.py:86
  294.6 3.3 collective-permute-start.3
  302.9 4.3 copy.231
  310.5 9.3 %reduce.69 = f32[2048,16]{1,0:T(8,128)S(1)} reduce(f32[2048,1,16]{2,1,0:T(1,128)S(1)} %bitcast.496, f32[]{:T(128)} %broadcast.556), dimensions={1}, to_apply=%bitcast.314.reduce_sub_computation | reduce | bytes 262148
  320.9 13.3 %all-to-all-start = ((f32[128,1,256]{2,1,0:T(1,128)}), f32[128,1,256]{2,1,0:T(1,128)S(1)}, u32[]{:S(2)}, u32[]{:S(2)}) async-start(f32[128,1,256]{2,1,0:T(1,128)} %reshape.1183), calls=%async_computation | async-start | bytes 262144 | tf_op jit(solution)/shard_map/all_to_all | solution.py:63
  334.4 97.6 %all-reduce.4 = (f32[3,3,4,64]{3,2,1,0:T(4,128)S(1)}, f32[64,64]{1,0:T(8,128)S(1)}, f32[64]{0:T(128)S(1)}) all-reduce(f32[3,3,4,64]{3,2,1,0:T(4,128)S(1)} %reduce_sum.27, f32[64,64]{1,0:T(8,128)S(1)} %reduce_sum.28, f32[64]{0:T(128)S(1)} %reduce_sum.29), channel_id=1, replica_groups=mesh['rep'=4,'sp'=128] {'rep','sp'}, use_global_device_ids=true, to_apply=%region_93.96 | all-reduce | flops 6464 | bytes 51712 | tf_op jit(solution)/shard_map/psum | solution.py:242
  442.9 9.3 %reduce.71 = f32[2048,16]{1,0:T(8,128)S(1)} reduce(f32[2048,1,16]{2,1,0:T(1,128)S(1)} %bitcast.497, f32[]{:T(128)} %broadcast.556), dimensions={1}, to_apply=%bitcast.316.reduce_sub_computation | reduce | bytes 262148
  453.2 9.4 %all-to-all-start.1 = ((f32[128,1,256]{2,1,0:T(1,128)}), f32[128,1,256]{2,1,0:T(1,128)S(1)}, u32[]{:S(2)}, u32[]{:S(2)}) async-start(f32[128,1,256]{2,1,0:T(1,128)} %reshape.1185), calls=%async_computation.1 | async-start | bytes 262144 | tf_op jit(solution)/shard_map/all_to_all | solution.py:63
  464.5 10.1 %all-to-all-done.1 = f32[128,1,256]{2,1,0:T(1,128)S(1)} async-done(((f32[128,1,256]{2,1,0:T(1,128)}), f32[128,1,256]{2,1,0:T(1,128)S(1)}, u32[]{:S(2)}, u32[]{:S(2)}) %all-to-all-start.1) | async-done | bytes 131104 | tf_op jit(solution)/shard_map/all_to_all | solution.py:63
  (539 shorter events, 207.2 us)
Async XLA Ops:
  0.6 27.3 %copy-start.22 = (f32[1,16,2048]{2,1,0:T(8,128)S(1)}, f32[1,16,2048]{2,1,0:T(8,128)}, u32[]{:S(2)}) copy-start(f32[1,16,2048]{2,1,0:T(8,128)} %param.117) | copy-start | bytes 393220
  1.7 27.1 %copy-start.20 = (f32[4,128,128]{2,1,0:T(8,128)S(1)}, f32[4,128,128]{2,1,0:T(8,128)}, u32[]{:S(2)}) copy-start(f32[4,128,128]{2,1,0:T(8,128)} %param.113) | copy-start | bytes 786436
  3.0 67.6 %collective-permute-start = (bf16[4,1,1,2048]{3,2,1,0:T(2,128)(2,1)S(1)}, bf16[4,1,1,2048]{3,2,1,0:T(2,128)(2,1)S(1)}, u32[]{:S(2)}, u32[]{:S(2)}) collective-permute-start(bf16[4,1,1,2048]{3,2,1,0:T(2,128)(2,1)S(1)} %get-tuple-element.1388), channel_id=1, source_target_pairs={{0,1},{1,2},{2,3},{3,4},{4,5},{5,6},{6,7},{7,8},{8,9},{9,10},{10,1... | collective-permute-start | bytes 49160 | tf_op jit(solution)/shard_map/ppermute | solution.py:19
  6.4 64.2 %collective-permute-start.1 = (bf16[4,1,1,2048]{3,2,1,0:T(2,128)(2,1)S(1)}, bf16[4,1,1,2048]{3,2,1,0:T(2,128)(2,1)S(1)}, u32[]{:S(2)}, u32[]{:S(2)}) collective-permute-start(bf16[4,1,1,2048]{3,2,1,0:T(2,128)(2,1)S(1)} %get-tuple-element.1389), channel_id=1, source_target_pairs={{1,0},{2,1},{3,2},{4,3},{5,4},{6,5},{7,6},{8,7},{9,8},{10,9},{11,1... | collective-permute-start | bytes 49160 | tf_op jit(solution)/shard_map/ppermute | solution.py:20
  19.4 61.3 %copy-start.60 = (s32[256]{0:T(256)}, s32[256]{0:T(256)S(1)}, u32[]{:S(2)}) copy-start(s32[256]{0:T(256)S(1)} %get-tuple-element.1420) | copy-start | bytes 3076
  35.1 28.9 %copy-start.62 = (s32[5]{0:T(128)S(1)}, s32[5]{0:T(128)}, u32[]{:S(2)}) copy-start(s32[5]{0:T(128)} %constant.563.clone.1) | copy-start | bytes 64
  35.1 35.3 %copy-start.5 = (bf16[64,64]{1,0:T(8,128)(2,1)S(1)}, bf16[64,64]{1,0:T(8,128)(2,1)}, u32[]{:S(2)}) copy-start(bf16[64,64]{1,0:T(8,128)(2,1)} %param.115) | copy-start | bytes 24580
  45.5 27.5 %all-to-all-start.2 = ((f32[128,1,256]{2,1,0:T(1,128)}), f32[128,1,256]{2,1,0:T(1,128)S(1)}, u32[]{:S(2)}, u32[]{:S(2)}) async-start(f32[128,1,256]{2,1,0:T(1,128)} %reshape.1187), calls=%async_computation.2 | async-start | bytes 262144 | tf_op jit(solution)/shard_map/all_to_all | solution.py:63
  61.2 17.3 %copy-start.32 = (s32[1024]{0:T(1024)}, s32[1024]{0:T(1024)S(1)}, u32[]{:S(2)}) copy-start(s32[1024]{0:T(1024)S(1)} %pad_clamp_fusion) | copy-start | bytes 12292
  64.0 16.7 %copy-start.41 = (pred[128]{0:T(512)(128)(4,1)}, pred[128]{0:T(512)(128)(4,1)S(1)}, u32[]{:S(2)}) copy-start(pred[128]{0:T(512)(128)(4,1)S(1)} %get-tuple-element.1409) | copy-start | bytes 388
  82.5 24.1 %copy-start.12 = (bf16[3,3,4,64]{3,2,1,0:T(4,128)(2,1)S(1)}, bf16[3,3,4,64]{3,2,1,0:T(4,128)(2,1)}, u32[]{:S(2)}) copy-start(bf16[3,3,4,64]{3,2,1,0:T(4,128)(2,1)} %param.114) | copy-start | bytes 13828
  82.5 24.1 %copy-start.26 = (bf16[64]{0:T(256)(128)(2,1)S(1)}, bf16[64]{0:T(256)(128)(2,1)}, u32[]{:S(2)}) copy-start(bf16[64]{0:T(256)(128)(2,1)} %param.116) | copy-start | bytes 388
  83.1 23.5 %copy-start.23 = (f32[4,1,16,512]{3,2,1,0:T(8,128)S(1)}, f32[4,1,16,512]{3,2,1,0:T(8,128)}, u32[]{:S(2)}) copy-start(f32[4,1,16,512]{3,2,1,0:T(8,128)} %custom-call.12) | copy-start | bytes 393220
  93.5 24.9 %all-to-all-start.3 = ((f32[128,1,256]{2,1,0:T(1,128)}), f32[128,1,256]{2,1,0:T(1,128)S(1)}, u32[]{:S(2)}, u32[]{:S(2)}) async-start(f32[128,1,256]{2,1,0:T(1,128)} %reshape.1189), calls=%async_computation.3 | async-start | bytes 262144 | tf_op jit(solution)/shard_map/all_to_all | solution.py:63
  147.4 16.5 %copy-start.4 = (bf16[4,4,1,18,514]{4,1,3,2,0:T(4,128)(2,1)S(1)}, bf16[4,4,1,18,514]{4,1,3,2,0:T(4,128)(2,1)}, u32[]{:S(2)}) copy-start(bf16[4,4,1,18,514]{4,1,3,2,0:T(4,128)(2,1)} %copy-done.3) | copy-start | bytes 888196 | tf_op jit(solution)/shard_map/while
  147.5 16.5 %copy-start.14 = (bf16[3,3,4,64]{3,2,1,0:T(4,128)(2,1)S(1)}, bf16[3,3,4,64]{3,2,1,0:T(4,128)(2,1)}, u32[]{:S(2)}) copy-start(bf16[3,3,4,64]{3,2,1,0:T(4,128)(2,1)} %copy-done.13) | copy-start | bytes 13828 | tf_op jit(solution)/shard_map/while
  147.5 16.5 %copy-start.28 = (bf16[64]{0:T(256)(128)(2,1)S(1)}, bf16[64]{0:T(256)(128)(2,1)}, u32[]{:S(2)}) copy-start(bf16[64]{0:T(256)(128)(2,1)} %copy-done.27) | copy-start | bytes 388 | tf_op jit(solution)/shard_map/while
  186.5 16.6 %copy-start.4 = (bf16[4,4,1,18,514]{4,1,3,2,0:T(4,128)(2,1)S(1)}, bf16[4,4,1,18,514]{4,1,3,2,0:T(4,128)(2,1)}, u32[]{:S(2)}) copy-start(bf16[4,4,1,18,514]{4,1,3,2,0:T(4,128)(2,1)} %copy-done.3) | copy-start | bytes 888196 | tf_op jit(solution)/shard_map/while
  186.5 16.5 %copy-start.14 = (bf16[3,3,4,64]{3,2,1,0:T(4,128)(2,1)S(1)}, bf16[3,3,4,64]{3,2,1,0:T(4,128)(2,1)}, u32[]{:S(2)}) copy-start(bf16[3,3,4,64]{3,2,1,0:T(4,128)(2,1)} %copy-done.13) | copy-start | bytes 13828 | tf_op jit(solution)/shard_map/while
  186.5 16.5 %copy-start.28 = (bf16[64]{0:T(256)(128)(2,1)S(1)}, bf16[64]{0:T(256)(128)(2,1)}, u32[]{:S(2)}) copy-start(bf16[64]{0:T(256)(128)(2,1)} %copy-done.27) | copy-start | bytes 388 | tf_op jit(solution)/shard_map/while
  186.5 16.5 %copy-start.30 = (s32[4]{0:T(128)S(1)}, s32[4]{0:T(128)}, u32[]{:S(2)}) copy-start(s32[4]{0:T(128)} %get-tuple-element.1712) | copy-start | bytes 52 | tf_op jit(solution)/shard_map/while
  225.5 16.5 %copy-start.4 = (bf16[4,4,1,18,514]{4,1,3,2,0:T(4,128)(2,1)S(1)}, bf16[4,4,1,18,514]{4,1,3,2,0:T(4,128)(2,1)}, u32[]{:S(2)}) copy-start(bf16[4,4,1,18,514]{4,1,3,2,0:T(4,128)(2,1)} %copy-done.3) | copy-start | bytes 888196 | tf_op jit(solution)/shard_map/while
  264.5 16.5 %copy-start.4 = (bf16[4,4,1,18,514]{4,1,3,2,0:T(4,128)(2,1)S(1)}, bf16[4,4,1,18,514]{4,1,3,2,0:T(4,128)(2,1)}, u32[]{:S(2)}) copy-start(bf16[4,4,1,18,514]{4,1,3,2,0:T(4,128)(2,1)} %copy-done.3) | copy-start | bytes 888196 | tf_op jit(solution)/shard_map/while
  264.5 16.5 %copy-start.14 = (bf16[3,3,4,64]{3,2,1,0:T(4,128)(2,1)S(1)}, bf16[3,3,4,64]{3,2,1,0:T(4,128)(2,1)}, u32[]{:S(2)}) copy-start(bf16[3,3,4,64]{3,2,1,0:T(4,128)(2,1)} %copy-done.13) | copy-start | bytes 13828 | tf_op jit(solution)/shard_map/while
  264.5 16.5 %copy-start.28 = (bf16[64]{0:T(256)(128)(2,1)S(1)}, bf16[64]{0:T(256)(128)(2,1)}, u32[]{:S(2)}) copy-start(bf16[64]{0:T(256)(128)(2,1)} %copy-done.27) | copy-start | bytes 388 | tf_op jit(solution)/shard_map/while
  292.0 15.8 %collective-permute-start.2 = (bf16[64,1,1,2048]{3,0,2,1:T(8,128)(2,1)S(1)}, bf16[64,1,1,2048]{3,0,2,1:T(8,128)(2,1)S(1)}, u32[]{:S(2)}, u32[]{:S(2)}) collective-permute-start(bf16[64,1,1,2048]{3,0,2,1:T(8,128)(2,1)S(1)} %get-tuple-element.1375), channel_id=1, source_target_pairs={{0,1},{1,2},{2,3},{3,4},{4,5},{5,6},{6,7},{7,8},{8,9},{9,10},{10,1... | collective-permute-start | bytes 786440 | tf_op jit(solution)/shard_map/ppermute | solution.py:19
  294.6 13.2 %collective-permute-start.3 = (bf16[64,1,1,2048]{3,0,2,1:T(8,128)(2,1)S(1)}, bf16[64,1,1,2048]{3,0,2,1:T(8,128)(2,1)S(1)}, u32[]{:S(2)}, u32[]{:S(2)}) collective-permute-start(bf16[64,1,1,2048]{3,0,2,1:T(8,128)(2,1)S(1)} %get-tuple-element.1376), channel_id=1, source_target_pairs={{1,0},{2,1},{3,2},{4,3},{5,4},{6,5},{7,6},{8,7},{9,8},{10,9},{11,1... | collective-permute-start | bytes 786440 | tf_op jit(solution)/shard_map/ppermute | solution.py:20
  309.9 24.4 %copy-start.61 = (f32[4,64]{1,0:T(4,128)S(1)}, f32[4,64]{1,0:T(4,128)}, u32[]{:S(2)}) copy-start(f32[4,64]{1,0:T(4,128)} %get-tuple-element.1699) | copy-start | bytes 3076
  309.9 24.4 %copy-start.25 = (f32[4,3,3,4,64]{4,3,2,1,0:T(4,128)S(1)}, f32[4,3,3,4,64]{4,3,2,1,0:T(4,128)}, u32[]{:S(2)}) copy-start(f32[4,3,3,4,64]{4,3,2,1,0:T(4,128)} %get-tuple-element.1697) | copy-start | bytes 110596
  310.5 23.8 %copy-start.21 = (f32[4,64,64]{2,1,0:T(8,128)S(1)}, f32[4,64,64]{2,1,0:T(8,128)}, u32[]{:S(2)}) copy-start(f32[4,64,64]{2,1,0:T(8,128)} %get-tuple-element.1698) | copy-start | bytes 196612
  320.9 111.7 %all-to-all-start = ((f32[128,1,256]{2,1,0:T(1,128)}), f32[128,1,256]{2,1,0:T(1,128)S(1)}, u32[]{:S(2)}, u32[]{:S(2)}) async-start(f32[128,1,256]{2,1,0:T(1,128)} %reshape.1183), calls=%async_computation | async-start | bytes 262144 | tf_op jit(solution)/shard_map/all_to_all | solution.py:63
  453.2 21.4 %all-to-all-start.1 = ((f32[128,1,256]{2,1,0:T(1,128)}), f32[128,1,256]{2,1,0:T(1,128)S(1)}, u32[]{:S(2)}, u32[]{:S(2)}) async-start(f32[128,1,256]{2,1,0:T(1,128)} %reshape.1185), calls=%async_computation.1 | async-start | bytes 262144 | tf_op jit(solution)/shard_map/all_to_all | solution.py:63
  (66 other events, 396.7 us)
where the time goes:
time: 496 us; the launch traced here: 487 us
  local copies, waits for them, and re-layouts  164 us (33%)
  blocking collectives  97.6 us (20%)
  other arithmetic  87.3 us (18%)
  starting transfers between devices  66.4 us (13%)
  matrix products  43.4 us (9%)
  waiting for transfers between devices  13.5 us (3%)
  between operations  12.5 us (3%)
    psum x1, blocking collectives, on_device(): lax.psum((conv_total, mixing_total, flux_total), ('rep', 'sp'))  97.6 us
    scatter-add x28, local copies, waits for them, and re-layouts, closure_backward(): piece_cot.at[:, :, row_tap:row_tap + rows, col_tap:col_tap + cols].add(term)  76.6 us
    all_to_all x4, starting transfers between devices, relayout(): moved = lax.all_to_all(field, 'sp', split_axis=2, concat_axis=1, tiled=True)  51.5 us
    unnamed x4, other arithmetic  37.3 us
    unnamed x119, local copies, waits for them, and re-layouts  13.9 us
    all_to_all x4, waiting for transfers between devices, relayout(): moved = lax.all_to_all(field, 'sp', split_axis=2, concat_axis=1, tiled=True)  13.5 us
    another operation x15, other arithmetic  12.7 us
    dot_general x4, matrix products, closure_backward(): jnp.einsum('orxy,prxy->op', first_act, pre_second_cot, preferred_element_...  12.4 us
  transfers between devices with their start and end apart: 8, of which 3 were waited for; matrix products, arithmetic and copies ran while one was open for 11% of the time, Pallas kernels for 0%

commit v1 on v0

--- a/solution.py
+++ b/solution.py
@@ -239,7 +239,9 @@
         inner = inner.at[:, :, -1].add(rim_terms(rims[:, :, 3], conv_weight, 0, side))
         feature_cot = inner.astype(jnp.bfloat16)
         grad = source_grad + feature_cot[0] + 2.0 * height * feature_cot[1]
-    conv_sum, mixing_sum, flux_sum = lax.psum((conv_total, mixing_total, flux_total), ("rep", "sp"))
+    conv_sum, mixing_sum, flux_sum = lax.psum(
+        lax.psum((conv_total, mixing_total, flux_total), "sp"), "rep"
+    )
     scale = 1.0 / math.sqrt(lax.axis_size("rep") * film_start.shape[0] * side * side)
     return (final_film, grad, conv_sum * scale, mixing_sum * scale, flux_sum * scale)
 

time: 496 us -> 1140 us (2.30)
  the two profiles are of different devices: /device:TPU:2 before, /device:TPU:1 now
where the time goes in v1:
time: 1140 us; the launch traced here: 1130 us
  blocking collectives  748 us (66%)
  local copies, waits for them, and re-layouts  164 us (14%)
  other arithmetic  87.5 us (8%)
  starting transfers between devices  63.6 us (6%)
  matrix products  42.1 us (4%)
  between operations  12.4 us (1%)
  waiting for transfers between devices  12.1 us (1%)
    psum x1, blocking collectives, on_device(): lax.psum((conv_total, mixing_total, flux_total), 'sp')  616 us
    psum x1, blocking collectives, on_device(): lax.psum(lax.psum((conv_total, mixing_total, flux_total), 'sp'), 'rep')  132 us
    scatter-add x28, local copies, waits for them, and re-layouts, closure_backward(): piece_cot.at[:, :, row_tap:row_tap + rows, col_tap:col_tap + cols].add(term)  76.6 us
    all_to_all x4, starting transfers between devices, relayout(): moved = lax.all_to_all(field, 'sp', split_axis=2, concat_axis=1, tiled=True)  54.8 us
    unnamed x4, other arithmetic  37.6 us
  transfers between devices with their start and end apart: 8, of which 3 were waited for; matrix products, arithmetic and copies ran while one was open for 5% of the time, Pallas kernels for 0%

profile of v1, /device:TPU:1, one launch (start us, length us, event | category | flops | bytes accessed | tf_op | source)
XLA Modules:
  0.0 1132.3 jit_solution(17907450745668953384)
XLA Ops:
  3.0 3.9 collective-permute-start
  9.2 3.2 sort.35
  12.4 3.2 sort.36
  30.6 9.4 reduce.65
  41.1 20.4 %all-to-all-start.2 = ((f32[128,1,256]{2,1,0:T(1,128)}), f32[128,1,256]{2,1,0:T(1,128)S(1)}, u32[]{:S(2)}, u32[]{:S(2)}) async-start(f32[128,1,256]{2,1,0:T(1,128)} %reshape.1187), calls=%async_computation.2 | async-start | bytes 262144 | tf_op jit(solution)/shard_map/all_to_all | solution.py:63
  82.9 9.4 reduce.67
  93.4 12.9 %all-to-all-start.3 = ((f32[128,1,256]{2,1,0:T(1,128)}), f32[128,1,256]{2,1,0:T(1,128)S(1)}, u32[]{:S(2)}, u32[]{:S(2)}) async-start(f32[128,1,256]{2,1,0:T(1,128)} %reshape.1189), calls=%async_computation.3 | async-start | bytes 262144 | tf_op jit(solution)/shard_map/all_to_all | solution.py:63
  106.4 7.4 while.44
  124.2 156.4 %while.45 = (s32[]{:T(128)}, f32[4,4,1,18,514]{4,1,3,2,0:T(4,128)}, f32[4,3,3,4,64]{4,3,2,1,0:T(4,128)}, f32[4,64,64]{2,1,0:T(8,128)}, f32[4,64]{1,0:T(4,128)}, ...) while((s32[]{:T(128)}, f32[4,4,1,18,514]{4,1,3,2,0:T(4,128)}, ...), condition=%wide.region_90.93_spmd, body=%wide.region_88.92_spmd.sunk | while | flops 327188544 | bytes 51537856 | solution.py:227
  132.8 3.1 fusion.288
  140.8 4.0 scatter-add.90
  146.8 4.1 scatter-add.91
  154.0 2.8 scatter-add.93
  171.8 3.1 fusion.288
  179.8 4.0 scatter-add.90
  185.8 4.1 scatter-add.91
  210.9 3.1 fusion.288
  218.9 4.0 scatter-add.90
  224.9 4.1 scatter-add.91
  249.9 3.1 fusion.288
  257.9 4.0 scatter-add.90
  263.9 4.1 scatter-add.91
  280.5 4.8 copy.228
  286.0 5.4 fusion.141
  300.1 4.3 copy.231
  307.7 9.4 reduce.69
  318.2 15.1 %all-to-all-start = ((f32[128,1,256]{2,1,0:T(1,128)}), f32[128,1,256]{2,1,0:T(1,128)S(1)}, u32[]{:S(2)}, u32[]{:S(2)}) async-start(f32[128,1,256]{2,1,0:T(1,128)} %reshape.1183), calls=%async_computation | async-start | bytes 262144 | tf_op jit(solution)/shard_map/all_to_all | solution.py:63
  333.4 616.0 %all-reduce.4 = (f32[3,3,4,64]{3,2,1,0:T(4,128)S(1)}, f32[64,64]{1,0:T(8,128)S(1)}, f32[64]{0:T(128)S(1)}) all-reduce(f32[3,3,4,64]{3,2,1,0:T(4,128)S(1)} %reduce_sum.27, f32[64,64]{1,0:T(8,128)S(1)} %reduce_sum.28, f32[64]{0:T(128)S(1)} %reduce_sum.29), channel_id=1, replica_groups=mesh['rep'=4,'sp'=128] {'sp'}, use_global_device_ids=true, to_apply=%region_93.96 | all-reduce | flops 6464 | bytes 51712 | tf_op jit(solution)/shard_map/psum | solution.py:243
  949.4 132.0 %all-reduce.5 = (f32[3,3,4,64]{3,2,1,0:T(4,128)S(1)}, f32[64,64]{1,0:T(8,128)S(1)}, f32[64]{0:T(128)S(1)}) all-reduce(f32[3,3,4,64]{3,2,1,0:T(4,128)S(1)} %get-tuple-element.1340, f32[64,64]{1,0:T(8,128)S(1)} %get-tuple-element.1341, f32[64]{0:T(128)S(1)} %get-tuple-element.1342), channel_id=1, replica_groups=mesh['rep'=4,'sp'=128] {'rep'}, use_global_device_ids=true, to_apply=%region_94.97 | all-reduce | flops 6464 | bytes 51712 | tf_op jit(solution)/shard_map/psum | solution.py:242
  1092.4 9.4 reduce.71
  1102.8 6.4 all-to-all-start.1
  1111.0 9.5 all-to-all-done.1
  (540 shorter events, 203.8 us)
Async XLA Ops:
  0.6 23.3 %copy-start.22 = (f32[1,16,2048]{2,1,0:T(8,128)S(1)}, f32[1,16,2048]{2,1,0:T(8,128)}, u32[]{:S(2)}) copy-start(f32[1,16,2048]{2,1,0:T(8,128)} %param.117) | copy-start | bytes 393220
  1.7 23.1 %copy-start.20 = (f32[4,128,128]{2,1,0:T(8,128)S(1)}, f32[4,128,128]{2,1,0:T(8,128)}, u32[]{:S(2)}) copy-start(f32[4,128,128]{2,1,0:T(8,128)} %param.113) | copy-start | bytes 786436
  3.0 67.8 %collective-permute-start = (bf16[4,1,1,2048]{3,2,1,0:T(2,128)(2,1)S(1)}, bf16[4,1,1,2048]{3,2,1,0:T(2,128)(2,1)S(1)}, u32[]{:S(2)}, u32[]{:S(2)}) collective-permute-start(bf16[4,1,1,2048]{3,2,1,0:T(2,128)(2,1)S(1)} %get-tuple-element.1391), channel_id=1, source_target_pairs={{0,1},{1,2},{2,3},{3,4},{4,5},{5,6},{6,7},{7,8},{8,9},{9,10},{10,1... | collective-permute-start | bytes 49160 | tf_op jit(solution)/shard_map/ppermute | solution.py:19
  6.9 63.9 %collective-permute-start.1 = (bf16[4,1,1,2048]{3,2,1,0:T(2,128)(2,1)S(1)}, bf16[4,1,1,2048]{3,2,1,0:T(2,128)(2,1)S(1)}, u32[]{:S(2)}, u32[]{:S(2)}) collective-permute-start(bf16[4,1,1,2048]{3,2,1,0:T(2,128)(2,1)S(1)} %get-tuple-element.1392), channel_id=1, source_target_pairs={{1,0},{2,1},{3,2},{4,3},{5,4},{6,5},{7,6},{8,7},{9,8},{10,9},{11,1... | collective-permute-start | bytes 49160 | tf_op jit(solution)/shard_map/ppermute | solution.py:20
  15.6 65.0 %copy-start.60 = (s32[256]{0:T(256)}, s32[256]{0:T(256)S(1)}, u32[]{:S(2)}) copy-start(s32[256]{0:T(256)S(1)} %get-tuple-element.1423) | copy-start | bytes 3076
  30.6 33.7 %copy-start.62 = (s32[5]{0:T(128)S(1)}, s32[5]{0:T(128)}, u32[]{:S(2)}) copy-start(s32[5]{0:T(128)} %constant.563.clone.1) | copy-start | bytes 64
  30.6 40.0 %copy-start.5 = (bf16[64,64]{1,0:T(8,128)(2,1)S(1)}, bf16[64,64]{1,0:T(8,128)(2,1)}, u32[]{:S(2)}) copy-start(bf16[64,64]{1,0:T(8,128)(2,1)} %param.115) | copy-start | bytes 24580
  41.1 31.7 %all-to-all-start.2 = ((f32[128,1,256]{2,1,0:T(1,128)}), f32[128,1,256]{2,1,0:T(1,128)S(1)}, u32[]{:S(2)}, u32[]{:S(2)}) async-start(f32[128,1,256]{2,1,0:T(1,128)} %reshape.1187), calls=%async_computation.2 | async-start | bytes 262144 | tf_op jit(solution)/shard_map/all_to_all | solution.py:63
  61.5 16.8 %copy-start.32 = (s32[1024]{0:T(1024)}, s32[1024]{0:T(1024)S(1)}, u32[]{:S(2)}) copy-start(s32[1024]{0:T(1024)S(1)} %pad_clamp_fusion) | copy-start | bytes 12292
  82.3 24.0 %copy-start.12 = (bf16[3,3,4,64]{3,2,1,0:T(4,128)(2,1)S(1)}, bf16[3,3,4,64]{3,2,1,0:T(4,128)(2,1)}, u32[]{:S(2)}) copy-start(bf16[3,3,4,64]{3,2,1,0:T(4,128)(2,1)} %param.114) | copy-start | bytes 13828
  82.3 24.0 %copy-start.26 = (bf16[64]{0:T(256)(128)(2,1)S(1)}, bf16[64]{0:T(256)(128)(2,1)}, u32[]{:S(2)}) copy-start(bf16[64]{0:T(256)(128)(2,1)} %param.116) | copy-start | bytes 388
  82.9 23.4 %copy-start.23 = (f32[4,1,16,512]{3,2,1,0:T(8,128)S(1)}, f32[4,1,16,512]{3,2,1,0:T(8,128)}, u32[]{:S(2)}) copy-start(f32[4,1,16,512]{3,2,1,0:T(8,128)} %custom-call.12) | copy-start | bytes 393220
  93.4 24.3 %all-to-all-start.3 = ((f32[128,1,256]{2,1,0:T(1,128)}), f32[128,1,256]{2,1,0:T(1,128)S(1)}, u32[]{:S(2)}, u32[]{:S(2)}) async-start(f32[128,1,256]{2,1,0:T(1,128)} %reshape.1189), calls=%async_computation.3 | async-start | bytes 262144 | tf_op jit(solution)/shard_map/all_to_all | solution.py:63
  146.8 16.6 %copy-start.4 = (bf16[4,4,1,18,514]{4,1,3,2,0:T(4,128)(2,1)S(1)}, bf16[4,4,1,18,514]{4,1,3,2,0:T(4,128)(2,1)}, u32[]{:S(2)}) copy-start(bf16[4,4,1,18,514]{4,1,3,2,0:T(4,128)(2,1)} %copy-done.3) | copy-start | bytes 888196 | tf_op jit(solution)/shard_map/while
  146.8 16.6 %copy-start.14 = (bf16[3,3,4,64]{3,2,1,0:T(4,128)(2,1)S(1)}, bf16[3,3,4,64]{3,2,1,0:T(4,128)(2,1)}, u32[]{:S(2)}) copy-start(bf16[3,3,4,64]{3,2,1,0:T(4,128)(2,1)} %copy-done.13) | copy-start | bytes 13828 | tf_op jit(solution)/shard_map/while
  185.8 16.6 %copy-start.4 = (bf16[4,4,1,18,514]{4,1,3,2,0:T(4,128)(2,1)S(1)}, bf16[4,4,1,18,514]{4,1,3,2,0:T(4,128)(2,1)}, u32[]{:S(2)}) copy-start(bf16[4,4,1,18,514]{4,1,3,2,0:T(4,128)(2,1)} %copy-done.3) | copy-start | bytes 888196 | tf_op jit(solution)/shard_map/while
  185.8 16.6 %copy-start.14 = (bf16[3,3,4,64]{3,2,1,0:T(4,128)(2,1)S(1)}, bf16[3,3,4,64]{3,2,1,0:T(4,128)(2,1)}, u32[]{:S(2)}) copy-start(bf16[3,3,4,64]{3,2,1,0:T(4,128)(2,1)} %copy-done.13) | copy-start | bytes 13828 | tf_op jit(solution)/shard_map/while
  185.8 16.6 %copy-start.28 = (bf16[64]{0:T(256)(128)(2,1)S(1)}, bf16[64]{0:T(256)(128)(2,1)}, u32[]{:S(2)}) copy-start(bf16[64]{0:T(256)(128)(2,1)} %copy-done.27) | copy-start | bytes 388 | tf_op jit(solution)/shard_map/while
  185.8 16.6 %copy-start.30 = (s32[4]{0:T(128)S(1)}, s32[4]{0:T(128)}, u32[]{:S(2)}) copy-start(s32[4]{0:T(128)} %get-tuple-element.1715) | copy-start | bytes 52 | tf_op jit(solution)/shard_map/while
  224.8 16.6 %copy-start.4 = (bf16[4,4,1,18,514]{4,1,3,2,0:T(4,128)(2,1)S(1)}, bf16[4,4,1,18,514]{4,1,3,2,0:T(4,128)(2,1)}, u32[]{:S(2)}) copy-start(bf16[4,4,1,18,514]{4,1,3,2,0:T(4,128)(2,1)} %copy-done.3) | copy-start | bytes 888196 | tf_op jit(solution)/shard_map/while
  224.9 16.6 %copy-start.14 = (bf16[3,3,4,64]{3,2,1,0:T(4,128)(2,1)S(1)}, bf16[3,3,4,64]{3,2,1,0:T(4,128)(2,1)}, u32[]{:S(2)}) copy-start(bf16[3,3,4,64]{3,2,1,0:T(4,128)(2,1)} %copy-done.13) | copy-start | bytes 13828 | tf_op jit(solution)/shard_map/while
  263.9 16.6 %copy-start.4 = (bf16[4,4,1,18,514]{4,1,3,2,0:T(4,128)(2,1)S(1)}, bf16[4,4,1,18,514]{4,1,3,2,0:T(4,128)(2,1)}, u32[]{:S(2)}) copy-start(bf16[4,4,1,18,514]{4,1,3,2,0:T(4,128)(2,1)} %copy-done.3) | copy-start | bytes 888196 | tf_op jit(solution)/shard_map/while
  263.9 16.6 %copy-start.14 = (bf16[3,3,4,64]{3,2,1,0:T(4,128)(2,1)S(1)}, bf16[3,3,4,64]{3,2,1,0:T(4,128)(2,1)}, u32[]{:S(2)}) copy-start(bf16[3,3,4,64]{3,2,1,0:T(4,128)(2,1)} %copy-done.13) | copy-start | bytes 13828 | tf_op jit(solution)/shard_map/while
  263.9 16.6 %copy-start.28 = (bf16[64]{0:T(256)(128)(2,1)S(1)}, bf16[64]{0:T(256)(128)(2,1)}, u32[]{:S(2)}) copy-start(bf16[64]{0:T(256)(128)(2,1)} %copy-done.27) | copy-start | bytes 388 | tf_op jit(solution)/shard_map/while
  263.9 16.6 %copy-start.30 = (s32[4]{0:T(128)S(1)}, s32[4]{0:T(128)}, u32[]{:S(2)}) copy-start(s32[4]{0:T(128)} %get-tuple-element.1715) | copy-start | bytes 52 | tf_op jit(solution)/shard_map/while
  291.5 13.5 %collective-permute-start.2 = (bf16[64,1,1,2048]{3,0,2,1:T(8,128)(2,1)S(1)}, bf16[64,1,1,2048]{3,0,2,1:T(8,128)(2,1)S(1)}, u32[]{:S(2)}, u32[]{:S(2)}) collective-permute-start(bf16[64,1,1,2048]{3,0,2,1:T(8,128)(2,1)S(1)} %get-tuple-element.1378), channel_id=1, source_target_pairs={{0,1},{1,2},{2,3},{3,4},{4,5},{5,6},{6,7},{7,8},{8,9},{9,10},{10,1... | collective-permute-start | bytes 786440 | tf_op jit(solution)/shard_map/ppermute | solution.py:19
  293.7 11.3 collective-permute-start.3
  307.1 26.2 %copy-start.61 = (f32[4,64]{1,0:T(4,128)S(1)}, f32[4,64]{1,0:T(4,128)}, u32[]{:S(2)}) copy-start(f32[4,64]{1,0:T(4,128)} %get-tuple-element.1702) | copy-start | bytes 3076
  307.1 26.2 %copy-start.25 = (f32[4,3,3,4,64]{4,3,2,1,0:T(4,128)S(1)}, f32[4,3,3,4,64]{4,3,2,1,0:T(4,128)}, u32[]{:S(2)}) copy-start(f32[4,3,3,4,64]{4,3,2,1,0:T(4,128)} %get-tuple-element.1700) | copy-start | bytes 110596
  307.7 25.7 %copy-start.21 = (f32[4,64,64]{2,1,0:T(8,128)S(1)}, f32[4,64,64]{2,1,0:T(8,128)}, u32[]{:S(2)}) copy-start(f32[4,64,64]{2,1,0:T(8,128)} %get-tuple-element.1701) | copy-start | bytes 196612
  318.2 763.9 %all-to-all-start = ((f32[128,1,256]{2,1,0:T(1,128)}), f32[128,1,256]{2,1,0:T(1,128)S(1)}, u32[]{:S(2)}, u32[]{:S(2)}) async-start(f32[128,1,256]{2,1,0:T(1,128)} %reshape.1183), calls=%async_computation | async-start | bytes 262144 | tf_op jit(solution)/shard_map/all_to_all | solution.py:63
  1102.8 17.7 %all-to-all-start.1 = ((f32[128,1,256]{2,1,0:T(1,128)}), f32[128,1,256]{2,1,0:T(1,128)S(1)}, u32[]{:S(2)}, u32[]{:S(2)}) async-start(f32[128,1,256]{2,1,0:T(1,128)} %reshape.1185), calls=%async_computation.1 | async-start | bytes 262144 | tf_op jit(solution)/shard_map/all_to_all | solution.py:63
  (66 other events, 385.6 us)
